TPU v7x, 512 devices: a whole 4x8x8 slice. The times are simulated.
512 devices in a mesh: row: 8 (over z), col: 16 (over y, core), vox: 4 (over x).
Axes of the slice: x: 4, y: 8, z: 8, core: 2. Of those that a mesh axis runs over, the one named last changes fastest.
Arguments:
- panel_top: bfloat16 [1024, 1024], P('row', ('col', 'vox')), may hold values from -0.059814453 to 0.059814453
- panel_low: bfloat16 [8192, 1024], P('row', ('col', 'vox')), may hold values from -1.1953125 to 1.1953125
- panel_next: bfloat16 [8192, 1024], P('row', ('col', 'vox')), may hold values from -1.1953125 to 1.1953125
- gram_rest: bfloat16 [8192, 8192], P('row', ('col', 'vox')), may hold values from -18 to 18
- inverses: bfloat16 [2, 1024, 1024], P(None, 'row'), as said below
- right_top: bfloat16 [2, 1024, 8192], P(None, None, ('col', 'vox')), may hold values from -1.796875 to 1.796875
- right_low: bfloat16 [8192, 8192], P('row', ('col', 'vox')), may hold values from -24 to 24
Outputs:
- factor: bfloat16 [2, 8192, 1024], P(None, 'row', ('col', 'vox'))
- solved: bfloat16 [2, 1024, 8192], P(None, None, ('col', 'vox'))
- trailing: float32 [8192, 8192], P('row', ('col', 'vox'))
- residual: float32 [8192, 8192], P('row', ('col', 'vox'))
Inputs may be any that keep to these rules, and one draw needn't show every extreme that they name: Each inverses[k] is lower triangular with diagonal entries from 1 to 2.
All inputs are finite; a program needn't handle non-finite values.
Results may differ from a plain program's by a relative error of at most 0.0057.
Values may be sent and summed in bfloat16 or wider, within the bound.
No kernel may reach another device: no remote copies, remote signals or barrier semaphores. Data moves between devices by JAX's collectives and lax.ppermute only.
A program may use at most 64 MiB of HBM per device.

v0:
```python
import jax
import jax.numpy as jnp
from jax import lax
from jax.sharding import PartitionSpec as P


def spread(block, axis, source):
    block = jnp.where(lax.axis_index(axis) == source, block, jnp.zeros_like(block))
    return lax.psum(block, axis)


def contract(left, right):
    return lax.dot_general(
        left, right, (((1,), (1,)), ((), ())), preferred_element_type=jnp.float32
    )


def per_device(panel_top, panel_low, panel_next, gram_rest, inverses, right_top, right_low):
    col_index = lax.axis_index(("col", "vox"))
    row_index = lax.axis_index("row")
    col_width = panel_low.shape[1]
    top_rows = panel_top.shape[0]
    low_rows = panel_low.shape[0]
    rest_cols = gram_rest.shape[1]
    root_row = col_index * rest_cols // low_rows
    whole_inverses = lax.all_gather(inverses, "row", axis=1, tiled=True)
    own_rows = lax.dynamic_slice_in_dim(whole_inverses, col_index * col_width, col_width, 1)
    rows_used = own_rows[0]
    own_top = contract(lax.all_gather(panel_top, ("col", "vox"), axis=1, tiled=True), rows_used)
    own_low = contract(lax.all_gather(panel_low, ("col", "vox"), axis=1, tiled=True), rows_used)
    first_top, first_low = (
        lax.all_gather(own_top.astype(jnp.bfloat16), ("col", "vox"), axis=1, tiled=True),
        lax.all_gather(own_low.astype(jnp.bfloat16), ("col", "vox"), axis=1, tiled=True),
    )
    outgoing = (
        lax.dynamic_slice_in_dim(
            first_top, col_index * col_width - root_row * top_rows, col_width, 0
        ),
        lax.dynamic_slice_in_dim(
            first_low, col_index * rest_cols - root_row * low_rows, rest_cols, 0
        ),
    )
    owner_top, owner_low = (
        spread(outgoing[0], "row", root_row),
        spread(outgoing[1], "row", root_row),
    )
    updated = (panel_next.astype(jnp.float32) - contract(first_low, owner_top)).astype(jnp.bfloat16)
    rows_used = own_rows[1]
    own_next = contract(lax.all_gather(updated, ("col", "vox"), axis=1, tiled=True), rows_used)
    second_low = lax.all_gather(own_next.astype(jnp.bfloat16), ("col", "vox"), axis=1, tiled=True)
    owner_next = spread(
        lax.dynamic_slice_in_dim(
            second_low, col_index * rest_cols - root_row * low_rows, rest_cols, 0
        ),
        "row",
        root_row,
    )
    trailing = (
        gram_rest.astype(jnp.float32)
        - contract(first_low, owner_low)
        - contract(second_low, owner_next)
    )
    first_solve = jnp.dot(
        whole_inverses[0], right_top[0], preferred_element_type=jnp.float32
    ).astype(jnp.bfloat16)
    top_slice = lax.dynamic_slice_in_dim(right_top[1], row_index * top_rows, top_rows, 0)
    top_part = (
        top_slice.astype(jnp.float32)
        - jnp.dot(first_top, first_solve, preferred_element_type=jnp.float32)
    ).astype(jnp.bfloat16)
    top_new = lax.all_gather(top_part, "row", axis=0, tiled=True)
    second_solve = jnp.dot(whole_inverses[1], top_new, preferred_element_type=jnp.float32).astype(
        jnp.bfloat16
    )
    residual = (
        right_low.astype(jnp.float32)
        - jnp.dot(first_low, first_solve, preferred_element_type=jnp.float32)
        - jnp.dot(second_low, second_solve, preferred_element_type=jnp.float32)
    )
    factor = jnp.stack(
        [
            lax.dynamic_slice_in_dim(first_low, col_index * col_width, col_width, 1),
            lax.dynamic_slice_in_dim(second_low, col_index * col_width, col_width, 1),
        ]
    )
    solved = jnp.stack([first_solve, second_solve])
    return (factor, solved, trailing, residual)


def solution(mesh):
    in_specs = (
        P("row", ("col", "vox")),
        P("row", ("col", "vox")),
        P("row", ("col", "vox")),
        P("row", ("col", "vox")),
        P(None, "row", None),
        P(None, None, ("col", "vox")),
        P("row", ("col", "vox")),
    )
    out_specs = (
        P(None, "row", ("col", "vox")),
        P(None, None, ("col", "vox")),
        P("row", ("col", "vox")),
        P("row", ("col", "vox")),
    )
    return jax.shard_map(
        per_device, mesh=mesh, in_specs=in_specs, out_specs=out_specs, check_vma=False
    )
```

profile of v0, /device:TPU:2, one launch (start us, length us, event | category | flops | bytes accessed | tf_op | source)
XLA Modules:
  0.0 587.9 jit_solution(6978349543570293704)
XLA Ops:
  8.0 0.7 all-gather.6.cloned.1.call-update
  8.7 88.6 %all-gather.8.cloned.1.call-done = bf16[1024,1024]{0,1:T(8,128)(2,1)} async-done(((bf16[1024,16]{0,1:T(8,128)(2,1)}), bf16[1024,1024]{0,1:T(8,128)(2,1)}) %all-gather.8.cloned.1.call-update) | async-done | bytes 2097168 | tf_op jit(solution)/shard_map/all_gather | solution.py:30
  97.4 59.5 %all-gather.6.cloned.1.call-done = bf16[2,1024,1024]{2,1,0:T(8,128)(2,1)} async-done(((bf16[2,128,1024]{2,1,0:T(8,128)(2,1)}), bf16[2,1024,1024]{2,1,0:T(8,128)(2,1)}) %all-gather.6.cloned.1.call-update) | async-done | bytes 4194320 | tf_op jit(solution)/shard_map/all_gather | solution.py:26
  156.9 2.6 fusion.6
  159.6 69.7 %all_gather.27 = bf16[128,1024]{0,1:T(8,128)(2,1)S(1)} all-gather(bf16[128,16]{0,1:T(8,128)(2,1)S(1)} %copy-done.7), channel_id=1, replica_groups=mesh['row'=8,'col'=16,'vox'=4] {'col','vox'}, dimensions={1}, use_global_device_ids=true | all-gather | bytes 266240 | tf_op jit(solution)/shard_map/all_gather | solution.py:29
  229.3 0.9 fusion.7
  230.2 66.4 %all_gather.28 = bf16[128,1024]{0,1:T(8,128)(2,1)S(1)} all-gather(bf16[128,16]{0,1:T(8,128)(2,1)S(1)} %fusion.7), channel_id=1, replica_groups=mesh['row'=8,'col'=16,'vox'=4] {'col','vox'}, dimensions={1}, use_global_device_ids=true | all-gather | bytes 266240 | tf_op jit(solution)/shard_map/all_gather | solution.py:32
  296.8 31.6 %psum.21 = bf16[16,1024]{0,1:T(8,128)(2,1)S(1)} all-reduce(bf16[16,1024]{0,1:T(8,128)(2,1)S(1)} %dynamic-slice_select_fusion.2), channel_id=1, replica_groups=mesh['row'=8,'col'=16,'vox'=4] {'row'}, use_global_device_ids=true, to_apply=%region_0.1 | all-reduce | flops 16384 | bytes 65536 | tf_op jit(solution)/shard_map/psum | solution.py:9
  328.4 2.7 fusion.4
  331.2 80.5 %all-gather.12.cloned.1.call-done = bf16[1024,1024]{0,1:T(8,128)(2,1)} async-done(((bf16[1024,16]{0,1:T(8,128)(2,1)}), bf16[1024,1024]{0,1:T(8,128)(2,1)}) %all-gather.12.cloned.1.call-update) | async-done | bytes 2097168 | tf_op jit(solution)/shard_map/all_gather | solution.py:49
  411.7 2.6 convolution_convert_fusion
  414.4 2.4 fusion.2
  417.2 26.8 %all_gather.31 = bf16[1024,128]{1,0:T(8,128)(2,1)S(1)} all-gather(bf16[128,128]{1,0:T(8,128)(2,1)S(1)} %fusion.5), channel_id=1, replica_groups=mesh['row'=8,'col'=16,'vox'=4] {'row'}, dimensions={0}, use_global_device_ids=true | all-gather | bytes 294912 | tf_op jit(solution)/shard_map/all_gather | solution.py:71
  444.0 0.7 fusion.3
  444.7 0.8 pad_maximum_fusion
  445.6 0.8 dynamic-slice_select_fusion.1
  446.3 0.7 convolution_subtract_fusion.1
  447.1 48.9 %all-gather.14.cloned.1.call-done = bf16[1024,1024]{0,1:T(8,128)(2,1)} async-done(((bf16[1024,16]{0,1:T(8,128)(2,1)}), bf16[1024,1024]{0,1:T(8,128)(2,1)}) %all-gather.14.cloned.1.call-update) | async-done | bytes 2097168 | tf_op jit(solution)/shard_map/all_gather | solution.py:50
  496.0 1.7 dynamic-slice_select_fusion
  497.7 0.8 dynamic-slice_bitcast_fusion.3
  499.1 3.2 convolution_subtract_fusion
  502.3 75.4 %all-reduce.3.cloned.1.call-done = (bf16[128,1024]{0,1:T(8,128)(2,1)}, bf16[128,1024]{0,1:T(8,128)(2,1)}) async-done(((bf16[128,1024]{0,1:T(8,128)(2,1)}, bf16[128,1024]{0,1:T(8,128)(2,1)}), (bf16[128,1024]{0,1:T(8,128)(2,1)}, bf16[128,1024]{0,1:T(8,128)(2,1)})) %all-reduce.3.cloned.1.call-update) | async-done | bytes 524304 | tf_op jit(solution)/shard_map/psum | solution.py:9
  577.6 1.8 convolution_subtract_fusion.3
  579.5 1.5 convolution_subtract_fusion.2
  (36 shorter events, 2.1 us)
Async XLA Ops:
  7.2 152.4 %copy-start.7 = (bf16[128,16]{0,1:T(8,128)(2,1)S(1)}, bf16[128,16]{0,1:T(8,128)(2,1)}, u32[]{:S(2)}) copy-start(bf16[128,16]{0,1:T(8,128)(2,1)} %param.7) | copy-start | bytes 12292
  7.2 90.2 %all-gather.8.cloned.1.call-start = ((), (), s32[]{:S(2)}) async-start(), calls=%async_computation.1 | async-start | bytes 2129920 | tf_op jit(solution)/shard_map/all_gather | solution.py:30
  7.9 149.0 %all-gather.6.cloned.1.call-start = ((), (), s32[]{:S(2)}) async-start(), calls=%async_computation | async-start | bytes 4718592 | tf_op jit(solution)/shard_map/all_gather | solution.py:26
  8.7 319.7 %copy-start.6 = (bf16[1024,16]{0,1:T(8,128)(2,1)S(1)}, bf16[1024,16]{0,1:T(8,128)(2,1)}, u32[]{:S(2)}) copy-start(bf16[1024,16]{0,1:T(8,128)(2,1)} %param.9) | copy-start | bytes 98308
  8.7 319.7 %all-gather.10.cloned.1.call-start = ((), (), s32[]{:S(2)}) async-start(), calls=%async_computation.2 | async-start | bytes 2129920 | tf_op jit(solution)/shard_map/all_gather | solution.py:33
  159.5 252.2 %all-gather.12.cloned.1.call-start = ((), (), s32[]{:S(2)}) async-start(), calls=%async_computation.3 | async-start | bytes 2129920 | tf_op jit(solution)/shard_map/all_gather | solution.py:49
  328.3 86.1 %copy-start.4 = (bf16[2,1024,128]{2,1,0:T(8,128)(2,1)S(1)}, bf16[2,1024,128]{2,1,0:T(8,128)(2,1)}, u32[]{:S(2)}) copy-start(bf16[2,1024,128]{2,1,0:T(8,128)(2,1)} %param.12) | copy-start | bytes 1572868
  331.1 164.9 %all-gather.14.cloned.1.call-start = ((), (), s32[]{:S(2)}) async-start(), calls=%async_computation.4 | async-start | bytes 2129920 | tf_op jit(solution)/shard_map/all_gather | solution.py:50
  414.3 163.3 %all-reduce.3.cloned.1.call-start = ((), (), s32[]{:S(2)}) async-start(), calls=%async_computation.5 | async-start | bytes 1048576 | tf_op jit(solution)/shard_map/psum | solution.py:9
  414.4 2.5 slice-start
  414.4 29.5 %copy-start.8 = (bf16[2,1024,1024]{2,1,0:T(8,128)(2,1)S(1)}, bf16[2,1024,1024]{2,1,0:T(8,128)(2,1)}, u32[]{:S(2)}) copy-start(bf16[2,1024,1024]{2,1,0:T(8,128)(2,1)} %all-gather.6.cloned.1.call-done) | copy-start | bytes 12582916
  444.0 1.6 copy-start
  444.0 2.4 copy-start.2
  499.1 78.6 %copy-start.3 = (bf16[1024,128]{1,0:T(8,128)(2,1)S(1)}, bf16[1024,128]{1,0:T(8,128)(2,1)}, u32[]{:S(2)}) copy-start(bf16[1024,128]{1,0:T(8,128)(2,1)} %param.10) | copy-start | bytes 786436
  577.6 1.8 copy-start.1
  577.6 1.9 copy-start.5
Sparse Core Ops, SparseCore 0:
  11.4 85.9 all-gather.7
  99.5 57.3 all-gather.5
  160.8 79.4 all-gather.9
  331.2 80.4 all-gather.11
  415.5 80.4 all-gather.13
  498.8 78.8 all-reduce.2
where the time goes:
time: 588 us
  waiting for transfers between devices  354 us (60%)
  blocking collectives  194 us (33%)
  matrix products  19.5 us (3%)
  between operations  14.3 us (2%)
    all_gather x1, waiting for transfers between devices, per_device(): lax.all_gather(panel_low, ('col', 'vox'), axis=1, tiled=True)  88.6 us
    all_gather x1, waiting for transfers between devices, per_device(): lax.all_gather(updated, ('col', 'vox'), axis=1, tiled=True)  80.5 us
    psum x1, waiting for transfers between devices, spread(): return lax.psum(block, axis)  75.4 us
    all_gather x1, blocking collectives, per_device(): lax.all_gather(panel_top, ('col', 'vox'), axis=1, tiled=True)  69.7 us
    all_gather x1, blocking collectives, per_device(): lax.all_gather(own_top.astype(jnp.bfloat16), ('col', 'vox'), axis=1, tile...  66.4 us
    all_gather x1, waiting for transfers between devices, per_device(): whole_inverses = lax.all_gather(inverses, 'row', axis=1, tiled=True)  59.5 us
    all_gather x1, waiting for transfers between devices, per_device(): lax.all_gather(own_next.astype(jnp.bfloat16), ('col', 'vox'), axis=1, til...  48.9 us
    psum x1, blocking collectives, spread(): return lax.psum(block, axis)  31.6 us
  transfers between devices with their start and end apart: 6, of which 5 were waited for; matrix products, arithmetic and copies ran while one was open for 2% of the time, Pallas kernels for 0%

commit v1 on v0

--- a/solution.py
+++ b/solution.py
@@ -2,6 +2,14 @@
 import jax.numpy as jnp
 from jax import lax
 from jax.sharding import PartitionSpec as P
+
+
+def tiled_gather(shard, axis, dim):
+    size = lax.axis_size(axis)
+    repeats = [size if d == dim else 1 for d in range(shard.ndim)]
+    return lax.all_to_all(
+        jnp.tile(shard, repeats), axis, split_axis=dim, concat_axis=dim, tiled=True
+    )
 
 
 def spread(block, axis, source):
@@ -46,7 +54,7 @@
     )
     updated = (panel_next.astype(jnp.float32) - contract(first_low, owner_top)).astype(jnp.bfloat16)
     rows_used = own_rows[1]
-    own_next = contract(lax.all_gather(updated, ("col", "vox"), axis=1, tiled=True), rows_used)
+    own_next = contract(tiled_gather(updated, ("col", "vox"), 1), rows_used)
     second_low = lax.all_gather(own_next.astype(jnp.bfloat16), ("col", "vox"), axis=1, tiled=True)
     owner_next = spread(
         lax.dynamic_slice_in_dim(

time: 588 us -> 564 us (0.959)
  waiting for transfers between devices: 354 us -> 321 us
  starting transfers between devices: 0.24 us -> 10.4 us
    all_gather x1 -> x0, waiting for transfers between devices: 80.5 us -> none  [per_device(): lax.all_gather(updated, ('col', 'vox'), axis=1, tiled=True)]
    all_to_all x0 -> x1, waiting for transfers between devices: none -> 51.2 us  [tiled_gather(): lax.all_to_all(jnp.tile(shard, repeats), axis, split_axis=dim, concat_axi...]
    all_to_all x0 -> x1, starting transfers between devices: none -> 10.2 us  [tiled_gather(): lax.all_to_all(jnp.tile(shard, repeats), axis, split_axis=dim, concat_axi...]
where the time goes in v1:
time: 564 us; the launch traced here: 563 us
  waiting for transfers between devices  321 us (57%)
  blocking collectives  193 us (34%)
  matrix products  18 us (3%)
  between operations  14 us (2%)
  starting transfers between devices  10.4 us (2%)
    all_gather x1, waiting for transfers between devices, per_device(): lax.all_gather(panel_low, ('col', 'vox'), axis=1, tiled=True)  88.6 us
    psum x1, waiting for transfers between devices, spread(): return lax.psum(block, axis)  75.4 us
    all_gather x1, blocking collectives, per_device(): lax.all_gather(panel_top, ('col', 'vox'), axis=1, tiled=True)  69.7 us
    all_gather x1, blocking collectives, per_device(): lax.all_gather(own_top.astype(jnp.bfloat16), ('col', 'vox'), axis=1, tile...  66.5 us
    all_gather x1, waiting for transfers between devices, per_device(): whole_inverses = lax.all_gather(inverses, 'row', axis=1, tiled=True)  59.5 us
    all_to_all x1, waiting for transfers between devices, tiled_gather(): lax.all_to_all(jnp.tile(shard, repeats), axis, split_axis=dim, concat_axi...  51.2 us
    all_gather x1, waiting for transfers between devices, per_device(): lax.all_gather(own_next.astype(jnp.bfloat16), ('col', 'vox'), axis=1, til...  45.2 us
    psum x1, blocking collectives, spread(): return lax.psum(block, axis)  31.5 us
  transfers between devices with their start and end apart: 6, of which 5 were waited for; matrix products, arithmetic and copies ran while one was open for 2% of the time, Pallas kernels for 0%

profile of v1, /device:TPU:2, one launch (start us, length us, event | category | flops | bytes accessed | tf_op | source)
XLA Modules:
  0.0 563.0 jit_solution(18259317767120465705)
XLA Ops:
  8.7 88.6 %all-gather.7.cloned.1.call-done = bf16[1024,1024]{0,1:T(8,128)(2,1)} async-done(((bf16[1024,16]{0,1:T(8,128)(2,1)}), bf16[1024,1024]{0,1:T(8,128)(2,1)}) %all-gather.7.cloned.1.call-update) | async-done | bytes 2097168 | tf_op jit(solution)/shard_map/all_gather | solution.py:38
  97.4 59.5 %all-gather.5.cloned.1.call-done = bf16[2,1024,1024]{2,1,0:T(8,128)(2,1)} async-done(((bf16[2,128,1024]{2,1,0:T(8,128)(2,1)}), bf16[2,1024,1024]{2,1,0:T(8,128)(2,1)}) %all-gather.5.cloned.1.call-update) | async-done | bytes 4194320 | tf_op jit(solution)/shard_map/all_gather | solution.py:34
  156.9 2.6 fusion.6
  159.5 69.7 %all_gather.24 = bf16[128,1024]{0,1:T(8,128)(2,1)S(1)} all-gather(bf16[128,16]{0,1:T(8,128)(2,1)S(1)} %copy-done.7), channel_id=1, replica_groups=mesh['row'=8,'col'=16,'vox'=4] {'col','vox'}, dimensions={1}, use_global_device_ids=true | all-gather | bytes 266240 | tf_op jit(solution)/shard_map/all_gather | solution.py:37
  229.3 0.9 fusion.7
  230.2 66.5 %all_gather.25 = bf16[128,1024]{0,1:T(8,128)(2,1)S(1)} all-gather(bf16[128,16]{0,1:T(8,128)(2,1)S(1)} %fusion.7), channel_id=1, replica_groups=mesh['row'=8,'col'=16,'vox'=4] {'col','vox'}, dimensions={1}, use_global_device_ids=true | all-gather | bytes 266240 | tf_op jit(solution)/shard_map/all_gather | solution.py:40
  296.8 31.5 %psum.21 = bf16[16,1024]{0,1:T(8,128)(2,1)S(1)} all-reduce(bf16[16,1024]{0,1:T(8,128)(2,1)S(1)} %dynamic-slice_select_fusion.2), channel_id=1, replica_groups=mesh['row'=8,'col'=16,'vox'=4] {'row'}, use_global_device_ids=true, to_apply=%region_0.1 | all-reduce | flops 16384 | bytes 65536 | tf_op jit(solution)/shard_map/psum | solution.py:17
  328.4 2.0 fusion.4
  330.4 1.6 tile.2
  332.0 10.2 %all-to-all-start = ((bf16[1024,64,16]{0,2,1:T(8,128)(2,1)}), bf16[1024,64,16]{0,2,1:T(8,128)(2,1)S(1)}, u32[]{:S(2)}, u32[]{:S(2)}) async-start(bf16[1024,64,16]{0,2,1:T(8,128)(2,1)} %tile.2), calls=%async_computation | async-start | bytes 4194304 | tf_op jit(solution)/shard_map/all_to_all | solution.py:10
  342.3 51.2 %all-to-all-done = bf16[1024,64,16]{0,2,1:T(8,128)(2,1)S(1)} async-done(((bf16[1024,64,16]{0,2,1:T(8,128)(2,1)}), bf16[1024,64,16]{0,2,1:T(8,128)(2,1)S(1)}, u32[]{:S(2)}, u32[]{:S(2)}) %all-to-all-start) | async-done | bytes 2097184 | tf_op jit(solution)/shard_map/all_to_all | solution.py:10
  393.5 1.8 convolution_convert_fusion
  395.4 2.4 fusion.2
  398.1 24.9 %all_gather.27 = bf16[1024,128]{1,0:T(8,128)(2,1)S(1)} all-gather(bf16[128,128]{1,0:T(8,128)(2,1)S(1)} %fusion.5), channel_id=1, replica_groups=mesh['row'=8,'col'=16,'vox'=4] {'row'}, dimensions={0}, use_global_device_ids=true | all-gather | bytes 294912 | tf_op jit(solution)/shard_map/all_gather | solution.py:79
  423.7 0.8 pad_maximum_fusion
  424.6 0.8 dynamic-slice_select_fusion.1
  425.4 0.7 convolution_subtract_fusion.1
  426.1 45.2 %all-gather.11.cloned.1.call-done = bf16[1024,1024]{0,1:T(8,128)(2,1)} async-done(((bf16[1024,16]{0,1:T(8,128)(2,1)}), bf16[1024,1024]{0,1:T(8,128)(2,1)}) %all-gather.11.cloned.1.call-update) | async-done | bytes 2097168 | tf_op jit(solution)/shard_map/all_gather | solution.py:58
  471.4 1.7 dynamic-slice_select_fusion
  473.1 0.8 dynamic-slice_bitcast_fusion.3
  474.5 3.2 convolution_subtract_fusion
  477.7 75.4 %all-reduce.3.cloned.1.call-done = (bf16[128,1024]{0,1:T(8,128)(2,1)}, bf16[128,1024]{0,1:T(8,128)(2,1)}) async-done(((bf16[128,1024]{0,1:T(8,128)(2,1)}, bf16[128,1024]{0,1:T(8,128)(2,1)}), (bf16[128,1024]{0,1:T(8,128)(2,1)}, bf16[128,1024]{0,1:T(8,128)(2,1)})) %all-reduce.3.cloned.1.call-update) | async-done | bytes 524304 | tf_op jit(solution)/shard_map/psum | solution.py:17
  553.0 1.8 convolution_subtract_fusion.3
  554.9 1.5 convolution_subtract_fusion.2
  (36 shorter events, 3.5 us)
Async XLA Ops:
  7.2 152.4 %copy-start.7 = (bf16[128,16]{0,1:T(8,128)(2,1)S(1)}, bf16[128,16]{0,1:T(8,128)(2,1)}, u32[]{:S(2)}) copy-start(bf16[128,16]{0,1:T(8,128)(2,1)} %param.7) | copy-start | bytes 12292
  7.2 90.2 %all-gather.7.cloned.1.call-start = ((), (), s32[]{:S(2)}) async-start(), calls=%async_computation.2 | async-start | bytes 2129920 | tf_op jit(solution)/shard_map/all_gather | solution.py:38
  7.9 149.0 %all-gather.5.cloned.1.call-start = ((), (), s32[]{:S(2)}) async-start(), calls=%async_computation.1 | async-start | bytes 4718592 | tf_op jit(solution)/shard_map/all_gather | solution.py:34
  8.7 319.7 %copy-start.6 = (bf16[1024,16]{0,1:T(8,128)(2,1)S(1)}, bf16[1024,16]{0,1:T(8,128)(2,1)}, u32[]{:S(2)}) copy-start(bf16[1024,16]{0,1:T(8,128)(2,1)} %param.9) | copy-start | bytes 98308
  8.7 319.7 %all-gather.9.cloned.1.call-start = ((), (), s32[]{:S(2)}) async-start(), calls=%async_computation.3 | async-start | bytes 2129920 | tf_op jit(solution)/shard_map/all_gather | solution.py:41
  332.0 61.5 %all-to-all-start = ((bf16[1024,64,16]{0,2,1:T(8,128)(2,1)}), bf16[1024,64,16]{0,2,1:T(8,128)(2,1)S(1)}, u32[]{:S(2)}, u32[]{:S(2)}) async-start(bf16[1024,64,16]{0,2,1:T(8,128)(2,1)} %tile.2), calls=%async_computation | async-start | bytes 4194304 | tf_op jit(solution)/shard_map/all_to_all | solution.py:10
  342.2 53.1 %copy-start.4 = (bf16[2,1024,128]{2,1,0:T(8,128)(2,1)S(1)}, bf16[2,1024,128]{2,1,0:T(8,128)(2,1)}, u32[]{:S(2)}) copy-start(bf16[2,1024,128]{2,1,0:T(8,128)(2,1)} %param.12) | copy-start | bytes 1572868
  342.2 129.1 %all-gather.11.cloned.1.call-start = ((), (), s32[]{:S(2)}) async-start(), calls=%async_computation.4 | async-start | bytes 2129920 | tf_op jit(solution)/shard_map/all_gather | solution.py:58
  395.3 157.7 %all-reduce.3.cloned.1.call-start = ((), (), s32[]{:S(2)}) async-start(), calls=%async_computation.5 | async-start | bytes 1048576 | tf_op jit(solution)/shard_map/psum | solution.py:17
  395.3 2.5 slice-start
  395.4 27.6 %copy-start.8 = (bf16[2,1024,1024]{2,1,0:T(8,128)(2,1)S(1)}, bf16[2,1024,1024]{2,1,0:T(8,128)(2,1)}, u32[]{:S(2)}) copy-start(bf16[2,1024,1024]{2,1,0:T(8,128)(2,1)} %all-gather.5.cloned.1.call-done) | copy-start | bytes 12582916
  423.0 1.6 copy-start
  423.0 2.4 copy-start.2
  474.5 78.5 %copy-start.3 = (bf16[1024,128]{1,0:T(8,128)(2,1)S(1)}, bf16[1024,128]{1,0:T(8,128)(2,1)}, u32[]{:S(2)}) copy-start(bf16[1024,128]{1,0:T(8,128)(2,1)} %param.10) | copy-start | bytes 786436
  553.0 1.8 copy-start.1
  553.0 1.9 copy-start.5
Sparse Core Ops, SparseCore 0:
  11.4 85.9 all-gather.6
  99.5 57.3 all-gather.4
  160.8 79.3 all-gather.8
  395.4 75.9 all-gather.10
  474.1 78.8 all-reduce.2
